TPU v7x, 256 devices: a whole 4x4x8 slice. The times are simulated.
256 devices in a mesh: section: 4 (over z_lo), rep: 8 (over y, core), tp: 8 (over z_hi, x).
Axes of the slice: x: 4, y: 4, z: 8 (z_hi: 2, z_lo: 4; z = z_hi * 4 + z_lo), core: 2. Of those that a mesh axis runs over, the one named last changes fastest.
Arguments:
- acts: bfloat16 [8, 256, 896], P('rep', None, 'tp'), may hold values from -6 to 6
- cotangent: bfloat16 [8, 256, 896], P('rep', None, 'tp'), may hold values from -8.5 to 8.5
- w_gate: bfloat16 [4, 8, 896, 4864], P('section', 'rep', None, 'tp'), may hold values from -3 to 3
- w_up: bfloat16 [4, 8, 896, 4864], P('section', 'rep', None, 'tp'), may hold values from -3 to 3
- w_down: bfloat16 [4, 8, 4864, 896], P('section', 'rep', 'tp'), may hold values from -4.2 to 4.2
- m_gate: bfloat16 [4, 8, 896, 4864], P('section', 'rep', None, 'tp'), may hold values from -0.099609375 to 0.099609375
- m_up: bfloat16 [4, 8, 896, 4864], P('section', 'rep', None, 'tp'), may hold values from -0.099609375 to 0.099609375
- m_down: bfloat16 [4, 8, 4864, 896], P('section', 'rep', 'tp'), may hold values from -0.099609375 to 0.099609375
- v_gate: bfloat16 [4, 8, 896, 4864], P('section', 'rep', None, 'tp'), may hold values from 0.0009994507 to 0.099609375
- v_up: bfloat16 [4, 8, 896, 4864], P('section', 'rep', None, 'tp'), may hold values from 0.0009994507 to 0.099609375
- v_down: bfloat16 [4, 8, 4864, 896], P('section', 'rep', 'tp'), may hold values from 0.0009994507 to 0.099609375
- steps: int32 [4], P('section'), may hold values from 0 to 999
Outputs:
- section_out: bfloat16 [4, 8, 256, 896], P('section', 'rep', None, 'tp')
- section_in_grad: bfloat16 [4, 8, 256, 896], P('section', 'rep', None, 'tp')
- new_gate: bfloat16 [4, 8, 896, 4864], P('section', 'rep', None, 'tp')
- new_up: bfloat16 [4, 8, 896, 4864], P('section', 'rep', None, 'tp')
- new_down: bfloat16 [4, 8, 4864, 896], P('section', 'rep', 'tp')
All inputs are finite; a program needn't handle non-finite values.
Results may differ from a plain program's by a relative error of at most 0.023.
Values may be sent and summed in bfloat16 or wider, within the bound.
A program may use at most 128 MiB of HBM per device.

v0:
```python
import functools
import math
import jax
import jax.numpy as jnp
from jax import lax
from jax.sharding import PartitionSpec as P

D = 896
FF = 4864
TOK = 128
MB = 2
NORM_EPS = 1e-06
ADAM_EPS = 1e-08
LEARN = 0.3
BETA_ONE = 0.9
BETA_TWO = 0.95


def as_sent(array):
    return jax.tree.map(lambda a: a.astype(jnp.bfloat16) if a.dtype == jnp.float32 else a, array)


def from_behind(array, axis, by):
    peers = lax.axis_size(axis)
    return lax.ppermute(array, axis, [(i, (i + by) % peers) for i in range(peers)])


def passed_along(value, axis, steps):
    count = lax.axis_size(axis)
    first, last = (max(0, -steps), min(count, count - steps))
    return lax.ppermute(value, axis, [(source, source + steps) for source in range(first, last)])


def widen(value):
    return lax.all_gather(value, "tp", axis=1, tiled=True)


def norm_parts(x_full):
    xf = x_full.astype(jnp.float32)
    rms = jnp.sqrt(jnp.mean(xf * xf, axis=1, keepdims=True) + NORM_EPS)
    normed = xf / rms
    normed_b = normed.astype(jnp.bfloat16)
    return (xf, rms, normed, normed_b)


def forward_parts(x_full, wg, wu):
    xf, rms, normed, normed_b = norm_parts(x_full)
    gate = jnp.dot(normed_b, wg, preferred_element_type=jnp.float32) * (1.0 / math.sqrt(D))
    upper = jnp.dot(normed_b, wu, preferred_element_type=jnp.float32) * (1.0 / math.sqrt(D))
    return (xf, rms, normed, normed_b, gate, upper)


def adam_step(weight, first, second, grad):
    m_new = BETA_ONE * first.astype(jnp.float32) + (1.0 - BETA_ONE) * grad
    v_new = BETA_TWO * second.astype(jnp.float32) + (1.0 - BETA_TWO) * grad * grad
    return (weight.astype(jnp.float32) - LEARN * m_new / (jnp.sqrt(v_new) + ADAM_EPS)).astype(
        jnp.bfloat16
    )


def partner_mean(stacked, distance):
    other = jax.tree.map(
        lambda part, own: part.astype(own.dtype),
        from_behind(as_sent(stacked), "rep", distance),
        stacked,
    )
    return ((stacked.astype(jnp.float32) + other.astype(jnp.float32)) * 0.5).astype(jnp.bfloat16)


def contract(left, right, left_dim, right_dim):
    return lax.dot_general(
        left, right, (((left_dim,), (right_dim,)), ((), ())), preferred_element_type=jnp.float32
    )


def on_device(
    acts, cotangent, w_gate, w_up, w_down, m_gate, m_up, m_down, v_gate, v_up, v_down, steps
):
    section = lax.axis_index("section")
    sections = lax.axis_size("section")
    part = lax.axis_index("tp")
    local_width = acts.shape[2]
    wg = w_gate[0, 0]
    wu = w_up[0, 0]
    wd = w_down[0, 0]
    local_hidden = wg.shape[1]
    inv_ff = 1.0 / math.sqrt(FF)
    ticks = MB + sections - 1
    inputs = acts[0].reshape(MB, TOK, local_width)
    cots = cotangent[0].reshape(MB, TOK, local_width)
    saved = jnp.zeros((MB, TOK, D), jnp.bfloat16)
    gate_saved = jnp.zeros((MB, TOK, local_hidden), jnp.float32)
    upper_saved = jnp.zeros((MB, TOK, local_hidden), jnp.float32)
    out_buf = jnp.zeros((MB, TOK, local_width), jnp.bfloat16)
    incoming = jnp.zeros((TOK, local_width), jnp.bfloat16)
    for tick in range(ticks):
        micro = tick - section
        valid = (micro >= 0) & (micro < MB)
        place = jnp.clip(micro, 0, MB - 1)
        first = lax.dynamic_index_in_dim(inputs, place, 0, keepdims=False)
        x_local = jnp.where(section == 0, first, incoming)
        x_full = widen(x_local)
        xf, rms, normed, normed_b, gate, upper = forward_parts(x_full, wg, wu)
        hidden = (jax.nn.silu(gate) * upper).astype(jnp.bfloat16)
        partial_out = jnp.dot(hidden, wd, preferred_element_type=jnp.float32) * inv_ff
        share = lax.psum_scatter(
            partial_out.astype(jnp.bfloat16), "tp", scatter_dimension=1, tiled=True
        ).astype(jnp.float32)
        y_local = (x_local.astype(jnp.float32) + share).astype(jnp.bfloat16)
        if tick < ticks - 1:
            incoming = passed_along(y_local, "section", 1)
        saved = jnp.where(valid, lax.dynamic_update_index_in_dim(saved, x_full, place, 0), saved)
        gate_saved = jnp.where(
            valid, lax.dynamic_update_index_in_dim(gate_saved, gate, place, 0), gate_saved
        )
        upper_saved = jnp.where(
            valid, lax.dynamic_update_index_in_dim(upper_saved, upper, place, 0), upper_saved
        )
        out_buf = jnp.where(
            valid, lax.dynamic_update_index_in_dim(out_buf, y_local, place, 0), out_buf
        )
    acc_gate = jnp.zeros(wg.shape, jnp.float32)
    acc_up = jnp.zeros(wu.shape, jnp.float32)
    acc_down = jnp.zeros(wd.shape, jnp.float32)
    grad_buf = jnp.zeros((MB, TOK, local_width), jnp.bfloat16)
    incoming_back = jnp.zeros((TOK, local_width), jnp.bfloat16)
    for tick in range(ticks):
        micro = tick - (sections - 1 - section)
        valid = (micro >= 0) & (micro < MB)
        place = jnp.clip(micro, 0, MB - 1)
        last_cot = lax.dynamic_index_in_dim(cots, place, 0, keepdims=False)
        dy_local = jnp.where(section == sections - 1, last_cot, incoming_back)
        dy_full = widen(dy_local)
        x_full = lax.dynamic_index_in_dim(saved, place, 0, keepdims=False)
        xf, rms, normed, normed_b = norm_parts(x_full)
        gate = lax.dynamic_index_in_dim(gate_saved, place, 0, keepdims=False)
        upper = lax.dynamic_index_in_dim(upper_saved, place, 0, keepdims=False)
        sig = jax.nn.sigmoid(gate)
        active = gate * sig
        hidden = (active * upper).astype(jnp.bfloat16)
        dh = contract(dy_full, wd, 1, 1) * inv_ff
        dgate = (dh * upper * sig * (1.0 + gate * (1.0 - sig))).astype(jnp.bfloat16)
        dup = (dh * active).astype(jnp.bfloat16)
        acc_down = acc_down + jnp.where(valid, contract(hidden, dy_full, 0, 0) * inv_ff, 0.0)
        acc_gate = acc_gate + jnp.where(
            valid, contract(normed_b, dgate, 0, 0) * (1.0 / math.sqrt(D)), 0.0
        )
        acc_up = acc_up + jnp.where(
            valid, contract(normed_b, dup, 0, 0) * (1.0 / math.sqrt(D)), 0.0
        )
        partial_in = (contract(dgate, wg, 1, 1) + contract(dup, wu, 1, 1)) * (1.0 / math.sqrt(D))
        dnorm_local = lax.psum_scatter(
            partial_in.astype(jnp.bfloat16), "tp", scatter_dimension=1, tiled=True
        ).astype(jnp.float32)
        normed_local = lax.dynamic_slice_in_dim(normed, part * local_width, local_width, 1)
        stat = lax.psum(jnp.sum(dnorm_local * normed_local, axis=1), "tp") / D
        dx_local = (
            dy_local.astype(jnp.float32) + (dnorm_local - normed_local * stat[:, None]) / rms
        ).astype(jnp.bfloat16)
        grad_buf = jnp.where(
            valid, lax.dynamic_update_index_in_dim(grad_buf, dx_local, place, 0), grad_buf
        )
        if tick < ticks - 1:
            incoming_back = passed_along(dx_local, "section", -1)
    new_gate_local = adam_step(wg, m_gate[0, 0], v_gate[0, 0], acc_gate)
    new_up_local = adam_step(wu, m_up[0, 0], v_up[0, 0], acc_up)
    new_down_local = adam_step(wd, m_down[0, 0], v_down[0, 0], acc_down)
    flat_size = wg.shape[0] * wg.shape[1]
    stacked = jnp.stack(
        [
            new_gate_local.reshape(flat_size),
            new_up_local.reshape(flat_size),
            new_down_local.reshape(flat_size),
        ]
    )
    levels = lax.axis_size("rep").bit_length() - 1
    branches = [functools.partial(partner_mean, distance=2**level) for level in range(levels)]
    which = steps[0] % levels
    averaged = lax.switch(which, branches, stacked)
    new_gate = averaged[0].reshape(wg.shape)[None, None]
    new_up = averaged[1].reshape(wu.shape)[None, None]
    new_down = averaged[2].reshape(wd.shape)[None, None]
    section_out = out_buf.reshape(1, 1, MB * TOK, local_width)
    section_in_grad = grad_buf.reshape(1, 1, MB * TOK, local_width)
    return (section_out, section_in_grad, new_gate, new_up, new_down)


def solution(mesh):
    return jax.shard_map(
        on_device,
        mesh=mesh,
        in_specs=(
            P("rep", None, "tp"),
            P("rep", None, "tp"),
            P("section", "rep", None, "tp"),
            P("section", "rep", None, "tp"),
            P("section", "rep", "tp", None),
            P("section", "rep", None, "tp"),
            P("section", "rep", None, "tp"),
            P("section", "rep", "tp", None),
            P("section", "rep", None, "tp"),
            P("section", "rep", None, "tp"),
            P("section", "rep", "tp", None),
            P("section"),
        ),
        out_specs=(
            P("section", "rep", None, "tp"),
            P("section", "rep", None, "tp"),
            P("section", "rep", None, "tp"),
            P("section", "rep", None, "tp"),
            P("section", "rep", "tp", None),
        ),
        check_vma=False,
    )
```

profile of v0, /device:TPU:66, one launch (start us, length us, event | category | flops | bytes accessed | tf_op | source)
XLA Modules:
  0.0 1532.5 jit_solution(6093599195167706535)
XLA Ops:
  9.0 44.1 %all-gather = bf16[1,128,896]{1,2,0:T(8,128)(2,1)S(1)} all-gather(bf16[1,128,112]{1,2,0:T(8,128)(2,1)S(1)} %copy_select_fusion.1), channel_id=2, replica_groups=mesh['section'=4,'rep'=8,'tp'=8] {'tp'}, dimensions={2}, use_global_device_ids=true | all-gather | bytes 258048 | tf_op jit(solution)/shard_map/all_gather | solution.py:35
  54.2 2.4 bitcast_dynamic-update-slice_fusion.1
  59.2 76.5 %reduce-scatter.11.cloned.1.call-done = bf16[128,112]{0,1:T(8,128)(2,1)} async-done(((bf16[128,896]{0,1:T(8,128)(2,1)}), bf16[128,112]{0,1:T(8,128)(2,1)}) %reduce-scatter.11.cloned.1.call-update) | async-done | bytes 28688 | tf_op jit(solution)/shard_map/reduce_scatter | solution.py:106
  136.5 2.6 collective-permute-start.3
  139.1 3.1 collective-permute-done.3
  142.3 40.6 %all_gather.31 = bf16[128,896]{0,1:T(8,128)(2,1)S(1)} all-gather(bf16[128,112]{0,1:T(8,128)(2,1)S(1)} %bitcast_select_fusion.19), channel_id=1, replica_groups=mesh['section'=4,'rep'=8,'tp'=8] {'tp'}, dimensions={1}, use_global_device_ids=true | all-gather | bytes 258048 | tf_op jit(solution)/shard_map/all_gather | solution.py:35
  183.5 2.2 fusion.134
  187.2 76.0 %reduce-scatter.13.cloned.1.call-done = bf16[128,112]{0,1:T(8,128)(2,1)} async-done(((bf16[128,896]{0,1:T(8,128)(2,1)}), bf16[128,112]{0,1:T(8,128)(2,1)}) %reduce-scatter.13.cloned.1.call-update) | async-done | bytes 28688 | tf_op jit(solution)/shard_map/reduce_scatter | solution.py:106
  264.0 2.6 collective-permute-start.4
  269.8 40.6 %all_gather.32 = bf16[128,896]{0,1:T(8,128)(2,1)S(1)} all-gather(bf16[128,112]{0,1:T(8,128)(2,1)S(1)} %bitcast_select_fusion.18), channel_id=1, replica_groups=mesh['section'=4,'rep'=8,'tp'=8] {'tp'}, dimensions={1}, use_global_device_ids=true | all-gather | bytes 258048 | tf_op jit(solution)/shard_map/all_gather | solution.py:35
  311.0 2.2 fusion.133
  315.4 75.3 %reduce-scatter.15.cloned.1.call-done = bf16[128,112]{0,1:T(8,128)(2,1)} async-done(((bf16[128,896]{0,1:T(8,128)(2,1)}), bf16[128,112]{0,1:T(8,128)(2,1)}) %reduce-scatter.15.cloned.1.call-update) | async-done | bytes 28688 | tf_op jit(solution)/shard_map/reduce_scatter | solution.py:106
  391.4 2.7 collective-permute-start.5
  394.1 43.8 %all-gather.1 = bf16[1,128,896]{1,2,0:T(8,128)(2,1)} all-gather(bf16[1,128,112]{1,2,0:T(8,128)(2,1)} %copy_select_fusion), channel_id=3, replica_groups=mesh['section'=4,'rep'=8,'tp'=8] {'tp'}, dimensions={2}, use_global_device_ids=true | all-gather | bytes 258048 | tf_op jit(solution)/shard_map/all_gather | solution.py:35
  439.4 44.0 %all_gather.33 = bf16[128,896]{0,1:T(8,128)(2,1)S(1)} all-gather(bf16[128,112]{0,1:T(8,128)(2,1)S(1)} %bitcast_select_fusion.17), channel_id=1, replica_groups=mesh['section'=4,'rep'=8,'tp'=8] {'tp'}, dimensions={1}, use_global_device_ids=true | all-gather | bytes 258048 | tf_op jit(solution)/shard_map/all_gather | solution.py:35
  484.0 2.2 fusion.132
  488.8 74.4 %reduce-scatter.17.cloned.1.call-done = bf16[128,112]{0,1:T(8,128)(2,1)} async-done(((bf16[128,896]{0,1:T(8,128)(2,1)}), bf16[128,112]{0,1:T(8,128)(2,1)}) %reduce-scatter.17.cloned.1.call-update) | async-done | bytes 28688 | tf_op jit(solution)/shard_map/reduce_scatter | solution.py:106
  564.0 2.7 collective-permute-start.6
  570.6 41.1 %all_gather.34 = bf16[128,896]{0,1:T(8,128)(2,1)S(1)} all-gather(bf16[128,112]{0,1:T(8,128)(2,1)S(1)} %bitcast_select_fusion.16), channel_id=1, replica_groups=mesh['section'=4,'rep'=8,'tp'=8] {'tp'}, dimensions={1}, use_global_device_ids=true | all-gather | bytes 258048 | tf_op jit(solution)/shard_map/all_gather | solution.py:35
  614.0 2.4 fusion.131
  623.4 2.7 fusion.36
  626.2 2.8 fusion.139
  630.5 69.0 %reduce-scatter.21.cloned.1.call-done = bf16[128,112]{0,1:T(8,128)(2,1)} async-done(((bf16[128,896]{0,1:T(8,128)(2,1)}), bf16[128,112]{0,1:T(8,128)(2,1)}) %reduce-scatter.21.cloned.1.call-update) | async-done | bytes 28688 | tf_op jit(solution)/shard_map/reduce_scatter | solution.py:152
  700.4 24.6 %psum.35 = f32[128]{0:T(128)S(1)} all-reduce(f32[128]{0:T(128)S(1)} %fusion.173), channel_id=1, replica_groups=mesh['section'=4,'rep'=8,'tp'=8] {'tp'}, use_global_device_ids=true, to_apply=%region_13.14 | all-reduce | flops 128 | bytes 1024 | tf_op jit(solution)/shard_map/psum | solution.py:156
  725.9 3.2 collective-permute-start.7
  729.2 47.1 %reduce-scatter.19.cloned.1.call-done = bf16[128,112]{0,1:T(8,128)(2,1)} async-done(((bf16[128,896]{0,1:T(8,128)(2,1)}), bf16[128,112]{0,1:T(8,128)(2,1)}) %reduce-scatter.19.cloned.1.call-update) | async-done | bytes 28688 | tf_op jit(solution)/shard_map/reduce_scatter | solution.py:106
  779.1 40.6 %all_gather.36 = bf16[128,896]{0,1:T(8,128)(2,1)S(1)} all-gather(bf16[128,112]{0,1:T(8,128)(2,1)S(1)} %bitcast_select_fusion.15), channel_id=1, replica_groups=mesh['section'=4,'rep'=8,'tp'=8] {'tp'}, dimensions={1}, use_global_device_ids=true | all-gather | bytes 258048 | tf_op jit(solution)/shard_map/all_gather | solution.py:35
  824.0 2.8 fusion.165
  826.8 2.9 fusion.143
  829.7 70.5 %reduce-scatter.23.cloned.1.call-done = bf16[128,112]{0,1:T(8,128)(2,1)} async-done(((bf16[128,896]{0,1:T(8,128)(2,1)}), bf16[128,112]{0,1:T(8,128)(2,1)}) %reduce-scatter.23.cloned.1.call-update) | async-done | bytes 28688 | tf_op jit(solution)/shard_map/reduce_scatter | solution.py:152
  901.0 24.6 %psum.36 = f32[128]{0:T(128)S(1)} all-reduce(f32[128]{0:T(128)S(1)} %fusion.177), channel_id=1, replica_groups=mesh['section'=4,'rep'=8,'tp'=8] {'tp'}, use_global_device_ids=true, to_apply=%region_17.18 | all-reduce | flops 128 | bytes 1024 | tf_op jit(solution)/shard_map/psum | solution.py:156
  926.6 3.3 collective-permute-start.8
  929.9 2.8 fusion.167
  933.3 39.7 %all_gather.37 = bf16[128,896]{0,1:T(8,128)(2,1)S(1)} all-gather(bf16[128,112]{0,1:T(8,128)(2,1)S(1)} %bitcast_select_fusion.14), channel_id=1, replica_groups=mesh['section'=4,'rep'=8,'tp'=8] {'tp'}, dimensions={1}, use_global_device_ids=true | all-gather | bytes 258048 | tf_op jit(solution)/shard_map/all_gather | solution.py:35
  977.1 2.7 fusion.161
  979.8 2.8 fusion.145
  982.6 75.5 %reduce-scatter.25.cloned.1.call-done = bf16[128,112]{0,1:T(8,128)(2,1)} async-done(((bf16[128,896]{0,1:T(8,128)(2,1)}), bf16[128,112]{0,1:T(8,128)(2,1)}) %reduce-scatter.25.cloned.1.call-update) | async-done | bytes 28688 | tf_op jit(solution)/shard_map/reduce_scatter | solution.py:152
  1059.0 24.6 %psum.37 = f32[128]{0:T(128)S(1)} all-reduce(f32[128]{0:T(128)S(1)} %fusion.181), channel_id=1, replica_groups=mesh['section'=4,'rep'=8,'tp'=8] {'tp'}, use_global_device_ids=true, to_apply=%region_21.22 | all-reduce | flops 128 | bytes 1024 | tf_op jit(solution)/shard_map/psum | solution.py:156
  1084.5 3.3 collective-permute-start.9
  1087.8 2.7 fusion.163
  1091.2 40.0 %all_gather.38 = bf16[128,896]{0,1:T(8,128)(2,1)S(1)} all-gather(bf16[128,112]{0,1:T(8,128)(2,1)S(1)} %bitcast_select_fusion.13), channel_id=1, replica_groups=mesh['section'=4,'rep'=8,'tp'=8] {'tp'}, dimensions={1}, use_global_device_ids=true | all-gather | bytes 258048 | tf_op jit(solution)/shard_map/all_gather | solution.py:35
  1135.3 2.7 fusion.157
  1138.0 2.9 fusion.147
  1140.9 75.4 %reduce-scatter.27.cloned.1.call-done = bf16[128,112]{0,1:T(8,128)(2,1)} async-done(((bf16[128,896]{0,1:T(8,128)(2,1)}), bf16[128,112]{0,1:T(8,128)(2,1)}) %reduce-scatter.27.cloned.1.call-update) | async-done | bytes 28688 | tf_op jit(solution)/shard_map/reduce_scatter | solution.py:152
  1217.2 24.6 %psum.38 = f32[128]{0:T(128)S(1)} all-reduce(f32[128]{0:T(128)S(1)} %fusion.185), channel_id=1, replica_groups=mesh['section'=4,'rep'=8,'tp'=8] {'tp'}, use_global_device_ids=true, to_apply=%region_25.26 | all-reduce | flops 128 | bytes 1024 | tf_op jit(solution)/shard_map/psum | solution.py:156
  1242.7 3.3 collective-permute-start.10
  1246.0 2.7 fusion.159
  1248.7 39.9 %all_gather.39 = bf16[128,896]{0,1:T(8,128)(2,1)S(1)} all-gather(bf16[128,112]{0,1:T(8,128)(2,1)S(1)} %bitcast_select_fusion.12), channel_id=1, replica_groups=mesh['section'=4,'rep'=8,'tp'=8] {'tp'}, dimensions={1}, use_global_device_ids=true | all-gather | bytes 258048 | tf_op jit(solution)/shard_map/all_gather | solution.py:35
  1292.2 7.5 fusion.21
  1299.7 3.1 copy.51
  1302.9 3.9 fusion.19
  1308.8 2.7 reshape.167
  1311.6 12.1 stack_reshape.10
  1323.6 4.9 fusion.20
  1330.1 4.0 reshape.169
  1334.0 11.3 stack_reshape.9
  1345.4 7.8 pad_maximum_fusion
  1353.2 138.0 %conditional.2 = (bf16[3,544768]{1,0:T(4,128)(2,1)}, bf16[1,544768]{1,0:T(2,128)(2,1)}, bf16[1,544768]{1,0:T(2,128)(2,1)}, bf16[1,544768]{1,0:T(2,128)(2,1)}, bf...) conditional(s32[]{:T(128)} %clamp.3, ...), branch_computations={%region_30.31_spmd, %region_31.32_spmd, %region_32.33_spmd} | conditional | flops 8171520 | bytes 56655996
  1354.3 10.7 collective-permute-start.2
  1365.0 81.6 %collective-permute-done.2 = bf16[3,544768]{1,0:T(4,128)(2,1)S(1)} collective-permute-done((bf16[3,544768]{1,0:T(4,128)(2,1)S(1)}, bf16[3,544768]{1,0:T(4,128)(2,1)S(1)}, u32[]{:S(2)}, u32[]{:S(2)}) %collective-permute-start.2) | collective-permute-done | bytes 3268640 | tf_op jit(solution)/shard_map/cond/branch_2_fun/ppermute | solution.py:25
  1446.6 2.9 add_multiply_fusion.2
  1449.5 32.6 %fusion.237 = (bf16[544768]{0:T(1024)(128)(2,1)S(1)}, bf16[1,544768]{1,0:T(2,128)(2,1)}, bf16[544768]{0:T(1024)(128)(2,1)}, bf16[1,544768]{1,0:T(2,128)(2,1)}, b...) fusion(bf16[3,544768]{1,0:T(4,128)(2,1)S(1)} %add_multiply_fusion.2), kind=kLoop, calls=%fused_computation.386 | loop fusion | bytes 9805824 | tf_op jit(solution)/shard_map/slice | solution.py:182
  1484.0 2.6 broadcast_in_dim_reshape_squeeze.28
  1492.3 31.5 %psum.39 = f32[128]{0:T(128)S(1)} all-reduce(f32[128]{0:T(128)S(1)} %fusion.189), channel_id=1, replica_groups=mesh['section'=4,'rep'=8,'tp'=8] {'tp'}, use_global_device_ids=true, to_apply=%region_29.30 | all-reduce | flops 128 | bytes 1024 | tf_op jit(solution)/shard_map/psum | solution.py:156
  (241 shorter events, 74.7 us)
Async XLA Ops:
  7.2 128.5 %reduce-scatter.11.cloned.1.call-start = ((), (), s32[]{:S(2)}) async-start(), calls=%async_computation.10 | async-start | bytes 258048 | tf_op jit(solution)/shard_map/reduce_scatter | solution.py:106
  53.3 3.3 copy-start.4
  59.2 124.3 %copy-start.3 = (bf16[1,1,896,608]{2,3,1,0:T(8,128)(2,1)S(1)}, bf16[1,1,896,608]{2,3,1,0:T(8,128)(2,1)}, u32[]{:S(2)}) copy-start(bf16[1,1,896,608]{2,3,1,0:T(8,128)(2,1)} %param.18) | copy-start | bytes 3268612
  59.2 204.0 %reduce-scatter.13.cloned.1.call-start = ((), (), s32[]{:S(2)}) async-start(), calls=%async_computation.11 | async-start | bytes 258048 | tf_op jit(solution)/shard_map/reduce_scatter | solution.py:106
  136.5 5.8 collective-permute-start.3
  182.9 2.9 copy-start.12
  183.5 2.3 copy-start.51
  187.1 203.6 %reduce-scatter.15.cloned.1.call-start = ((), (), s32[]{:S(2)}) async-start(), calls=%async_computation.12 | async-start | bytes 258048 | tf_op jit(solution)/shard_map/reduce_scatter | solution.py:106
  264.0 5.8 collective-permute-start.4
  267.6 47.0 %copy-start.26 = (bf16[1,128,112]{1,0,2:T(2,128)(2,1)}, bf16[1,128,112]{1,0,2:T(2,128)(2,1)S(1)}, u32[]{:S(2)}) copy-start(bf16[1,128,112]{1,0,2:T(2,128)(2,1)S(1)} %get-tuple-element.116) | copy-start | bytes 86020
  269.8 43.5 %copy-start.34 = (bf16[128,112]{0,1:T(8,128)(2,1)}, bf16[128,112]{0,1:T(8,128)(2,1)S(1)}, u32[]{:S(2)}) copy-start(bf16[128,112]{0,1:T(8,128)(2,1)S(1)} %bitcast_select_fusion.18) | copy-start | bytes 86020
  310.4 2.9 copy-start.14
  311.0 2.3 copy-start.52
  314.6 248.6 %reduce-scatter.17.cloned.1.call-start = ((), (), s32[]{:S(2)}) async-start(), calls=%async_computation.13 | async-start | bytes 258048 | tf_op jit(solution)/shard_map/reduce_scatter | solution.py:106
  391.4 47.2 %collective-permute-start.5 = (bf16[128,112]{0,1:T(8,128)(2,1)S(1)}, bf16[128,112]{0,1:T(8,128)(2,1)S(1)}, u32[]{:S(2)}, u32[]{:S(2)}) collective-permute-start(bf16[128,112]{0,1:T(8,128)(2,1)S(1)} %get-tuple-element.80), channel_id=1, source_target_pairs={{0,64},{64,128},{128,192},{1,65},{65,129},{129,193},{2,66},{66,130... | collective-permute-start | bytes 86024 | tf_op jit(solution)/shard_map/ppermute | solution.py:31
  439.4 44.1 %copy-start.33 = (bf16[128,112]{0,1:T(8,128)(2,1)}, bf16[128,112]{0,1:T(8,128)(2,1)S(1)}, u32[]{:S(2)}) copy-start(bf16[128,112]{0,1:T(8,128)(2,1)S(1)} %bitcast_select_fusion.17) | copy-start | bytes 86020
  483.4 2.9 copy-start.15
  484.0 2.3 copy-start.53
  487.6 212.0 %reduce-scatter.21.cloned.1.call-start = ((), (), s32[]{:S(2)}) async-start(), calls=%async_computation.15 | async-start | bytes 258048 | tf_op jit(solution)/shard_map/reduce_scatter | solution.py:152
  564.0 50.0 %copy-start.18 = (bf16[2,128,112]{1,2,0:T(8,128)(2,1)}, bf16[2,128,112]{1,2,0:T(8,128)(2,1)S(1)}, u32[]{:S(2)}) copy-start(bf16[2,128,112]{1,2,0:T(8,128)(2,1)S(1)} %get-tuple-element.77) | copy-start | bytes 172036
  564.0 5.8 collective-permute-start.6
  570.6 41.2 %copy-start.28 = (bf16[128,112]{0,1:T(8,128)(2,1)}, bf16[128,112]{0,1:T(8,128)(2,1)S(1)}, u32[]{:S(2)}) copy-start(bf16[128,112]{0,1:T(8,128)(2,1)S(1)} %bitcast_select_fusion.16) | copy-start | bytes 86020
  614.0 2.4 copy-start.17
  614.0 2.4 copy-start.54
  618.4 10.7 copy-start.43
  618.4 10.7 copy-start.44
  620.2 3.2 copy-start.47
  620.2 3.2 copy-start.48
  622.0 4.1 copy-start.49
  623.3 152.9 %reduce-scatter.19.cloned.1.call-start = ((), (), s32[]{:S(2)}) async-start(), calls=%async_computation.14 | async-start | bytes 258048 | tf_op jit(solution)/shard_map/reduce_scatter | solution.py:106
  626.1 4.4 copy-start.45
  629.0 96.1 %copy-start.27 = (bf16[1,128,112]{1,0,2:T(2,128)(2,1)S(1)}, bf16[1,128,112]{1,0,2:T(2,128)(2,1)}, u32[]{:S(2)}) copy-start(bf16[1,128,112]{1,0,2:T(2,128)(2,1)} %copy-done.26) | copy-start | bytes 86020
  629.0 147.2 %copy-start.19 = (bf16[2,128,112]{1,2,0:T(8,128)(2,1)S(1)}, bf16[2,128,112]{1,2,0:T(8,128)(2,1)}, u32[]{:S(2)}) copy-start(bf16[2,128,112]{1,2,0:T(8,128)(2,1)} %copy-done.18) | copy-start | bytes 172036
  629.0 147.2 %copy-start.29 = (bf16[128,112]{0,1:T(8,128)(2,1)S(1)}, bf16[128,112]{0,1:T(8,128)(2,1)}, u32[]{:S(2)}) copy-start(bf16[128,112]{0,1:T(8,128)(2,1)} %copy-done.28) | copy-start | bytes 86020
  629.0 148.7 %copy-start.39 = (bf16[1,128,112]{1,0,2:T(2,128)(2,1)S(1)}, bf16[1,128,112]{1,0,2:T(2,128)(2,1)}, u32[]{:S(2)}) copy-start(bf16[1,128,112]{1,0,2:T(2,128)(2,1)} %get-tuple-element.115) | copy-start | bytes 86020
  629.0 271.1 %reduce-scatter.23.cloned.1.call-start = ((), (), s32[]{:S(2)}) async-start(), calls=%async_computation.16 | async-start | bytes 258048 | tf_op jit(solution)/shard_map/reduce_scatter | solution.py:152
  725.9 51.8 %collective-permute-start.7 = (bf16[128,112]{0,1:T(8,128)(2,1)S(1)}, bf16[128,112]{0,1:T(8,128)(2,1)}, u32[]{:S(2)}, u32[]{:S(2)}) collective-permute-start(bf16[128,112]{0,1:T(8,128)(2,1)S(1)} %get-tuple-element.76), channel_id=1, source_target_pairs={{64,0},{128,64},{192,128},{65,1},{129,65},{193,129},{66,2},{130,66... | collective-permute-start | bytes 86024 | tf_op jit(solution)/shard_map/ppermute | solution.py:31
  824.0 234.1 %reduce-scatter.25.cloned.1.call-start = ((), (), s32[]{:S(2)}) async-start(), calls=%async_computation.17 | async-start | bytes 258048 | tf_op jit(solution)/shard_map/reduce_scatter | solution.py:152
  829.7 103.0 %copy-start.38 = (bf16[1,128,112]{1,0,2:T(2,128)(2,1)S(1)}, bf16[1,128,112]{1,0,2:T(2,128)(2,1)}, u32[]{:S(2)}) copy-start(bf16[1,128,112]{1,0,2:T(2,128)(2,1)} %get-tuple-element.114) | copy-start | bytes 86020
  925.6 47.4 %copy-start.55 = (bf16[1,1,608,896]{3,2,1,0:T(8,128)(2,1)S(1)}, bf16[1,1,608,896]{3,2,1,0:T(8,128)(2,1)}, u32[]{:S(2)}) copy-start(bf16[1,1,608,896]{3,2,1,0:T(8,128)(2,1)} %param.19) | copy-start | bytes 3268612
  926.6 6.1 collective-permute-start.8
  977.0 239.3 %reduce-scatter.27.cloned.1.call-start = ((), (), s32[]{:S(2)}) async-start(), calls=%async_computation.18 | async-start | bytes 258048 | tf_op jit(solution)/shard_map/reduce_scatter | solution.py:152
  982.6 108.0 %copy-start.37 = (bf16[1,128,112]{1,0,2:T(2,128)(2,1)S(1)}, bf16[1,128,112]{1,0,2:T(2,128)(2,1)}, u32[]{:S(2)}) copy-start(bf16[1,128,112]{1,0,2:T(2,128)(2,1)} %get-tuple-element.113) | copy-start | bytes 86020
  1083.6 47.6 %copy-start.56 = (bf16[1,1,608,896]{3,2,1,0:T(8,128)(2,1)S(1)}, bf16[1,1,608,896]{3,2,1,0:T(8,128)(2,1)}, u32[]{:S(2)}) copy-start(bf16[1,1,608,896]{3,2,1,0:T(8,128)(2,1)} %param.19) | copy-start | bytes 3268612
  1084.5 6.0 collective-permute-start.9
  1135.2 356.1 %reduce-scatter.29.cloned.1.call-start = ((), (), s32[]{:S(2)}) async-start(), calls=%async_computation.19 | async-start | bytes 258048 | tf_op jit(solution)/shard_map/reduce_scatter | solution.py:152
  1140.9 107.9 %copy-start.36 = (bf16[1,128,112]{1,0,2:T(2,128)(2,1)S(1)}, bf16[1,128,112]{1,0,2:T(2,128)(2,1)}, u32[]{:S(2)}) copy-start(bf16[1,128,112]{1,0,2:T(2,128)(2,1)} %get-tuple-element.112) | copy-start | bytes 86020
  1241.7 46.9 %copy-start.57 = (bf16[1,1,608,896]{3,2,1,0:T(8,128)(2,1)S(1)}, bf16[1,1,608,896]{3,2,1,0:T(8,128)(2,1)}, u32[]{:S(2)}) copy-start(bf16[1,1,608,896]{3,2,1,0:T(8,128)(2,1)} %param.19) | copy-start | bytes 3268612
  1242.7 6.0 collective-permute-start.10
  1292.1 10.7 copy-start.9
  1292.1 10.7 copy-start.10
  1292.1 10.7 copy-start.11
  1292.2 10.7 copy-start.58
  1292.2 10.7 copy-start.59
  1299.7 3.1 copy-start.8
  1299.7 3.1 copy-start.41
  1299.7 3.1 copy-start.46
  1311.6 12.1 copy-start.7
  1311.6 12.1 copy-start.60
  1330.1 15.3 %copy-start.6 = (bf16[1,544768]{1,0:T(2,128)(2,1)S(1)}, bf16[1,544768]{1,0:T(2,128)(2,1)}, u32[]{:S(2)}) copy-start(bf16[1,544768]{1,0:T(2,128)(2,1)} %stack_reshape.10) | copy-start | bytes 3268612
  1334.0 11.4 copy-start.5
  1354.3 92.3 %collective-permute-start.2 = (bf16[3,544768]{1,0:T(4,128)(2,1)S(1)}, bf16[3,544768]{1,0:T(4,128)(2,1)S(1)}, u32[]{:S(2)}, u32[]{:S(2)}) collective-permute-start(bf16[3,544768]{1,0:T(4,128)(2,1)S(1)} %param.2), channel_id=1, source_target_pairs={{0,32},{8,40},{16,48},{24,56},{32,0},{40,8},{48,16},{56,24},{1,33}... | collective-permute-start | bytes 9805832 | tf_op jit(solution)/shard_map/cond/branch_2_fun/ppermute | solution.py:25
  1449.5 32.6 %copy-start.2 = (bf16[3,544768]{1,0:T(4,128)(2,1)}, bf16[3,544768]{1,0:T(4,128)(2,1)S(1)}, u32[]{:S(2)}) copy-start(bf16[3,544768]{1,0:T(4,128)(2,1)S(1)} %add_multiply_fusion.2) | copy-start | bytes 9805828 | tf_op jit(solution)/shard_map/conditional
  1491.3 34.2 %copy-start.16 = (bf16[1,1,896,608]{2,3,1,0:T(8,128)(2,1)}, bf16[1,1,896,608]{2,3,1,0:T(8,128)(2,1)S(1)}, u32[]{:S(2)}) copy-start(bf16[1,1,896,608]{2,3,1,0:T(8,128)(2,1)S(1)} %get-tuple-element.44) | copy-start | bytes 3268612
  (14 other events, 13.7 us)
Sparse Core Ops, SparseCore 0:
  59.3 76.3 reduce-scatter.10
  187.2 75.9 reduce-scatter.12
  314.7 75.9 reduce-scatter.14
  487.7 75.4 reduce-scatter.16
  623.5 76.0 reduce-scatter.20
  703.1 73.1 reduce-scatter.18
  824.1 76.0 reduce-scatter.22
  977.2 80.9 reduce-scatter.24
  1135.3 80.9 reduce-scatter.26
  1292.2 80.7 reduce-scatter.28
where the time goes:
time: 1540 us; the launch traced here: 1530 us
  waiting for transfers between devices  729 us (47%)
  blocking collectives  544 us (35%)
  local copies, waits for them, and re-layouts  88.1 us (6%)
  matrix products  87.2 us (6%)
  starting transfers between devices  34.7 us (2%)
  other arithmetic  32.1 us (2%)
  between operations  16 us (1%)
    all_gather x10, blocking collectives, widen(): return lax.all_gather(value, 'tp', axis=1, tiled=True)  414 us
    reduce_scatter x5, waiting for transfers between devices, on_device(): lax.psum_scatter(partial_out.astype(jnp.bfloat16), 'tp', scatter_dimensio...  349 us
    reduce_scatter x5, waiting for transfers between devices, on_device(): lax.psum_scatter(partial_in.astype(jnp.bfloat16), 'tp', scatter_dimension...  290 us
    psum x5, blocking collectives, on_device(): stat = lax.psum(jnp.sum(dnorm_local * normed_local, axis=1), 'tp') / D  130 us
    ppermute x1, waiting for transfers between devices, from_behind(): lax.ppermute(array, axis, [(i, (i + by) % peers) for i in range(peers)])  81.6 us
    dot_general x30, matrix products, contract(): lax.dot_general(left, right, (((left_dim,), (right_dim,)), ((), ())), pre...  64.8 us
    slice x1, local copies, waits for them, and re-layouts, on_device(): new_down = averaged[2].reshape(wd.shape)[None, None]  32.6 us
  transfers between devices with their start and end apart: 19, of which 13 were waited for; matrix products, arithmetic and copies ran while one was open for 9% of the time, Pallas kernels for 0%

commit v1 on v0

--- a/solution.py
+++ b/solution.py
@@ -32,7 +32,14 @@
 
 
 def widen(value):
-    return lax.all_gather(value, "tp", axis=1, tiled=True)
+
+    def wrap_the_joints(local_x, row_axis):
+        tile_out = lax.axis_size(row_axis)
+        mid_arr = jnp.stack([local_x] * tile_out)
+        n_now = lax.all_to_all(mid_arr, row_axis, 0, 0)
+        return jnp.concatenate(n_now, axis=1)
+
+    return wrap_the_joints(value, "tp")
 
 
 def norm_parts(x_full):

time: 1540 us -> 1300 us (0.84)
  blocking collectives: 544 us -> 143 us
  waiting for transfers between devices: 729 us -> 800 us
  starting transfers between devices: 34.7 us -> 101 us
    all_gather x10 -> x0, blocking collectives: 414 us -> none  [widen(): return lax.all_gather(value, 'tp', axis=1, tiled=True)]
    all_to_all x0 -> x9, starting transfers between devices: none -> 66.3 us  [wrap_the_joints(): n_now = lax.all_to_all(mid_arr, row_axis, 0, 0)]
    all_to_all x0 -> x9, waiting for transfers between devices: none -> 63.2 us  [wrap_the_joints(): n_now = lax.all_to_all(mid_arr, row_axis, 0, 0)]
    all_to_all x0 -> x1, blocking collectives: none -> 18.1 us  [wrap_the_joints(): n_now = lax.all_to_all(mid_arr, row_axis, 0, 0)]
  transfers between devices with their start and end apart: 19 -> 28, of which waited for: 13 -> 24; matrix products, arithmetic and copies ran while one was open for 9% -> 13% of each run, Pallas kernels for 0% -> 0%
where the time goes in v1:
time: 1300 us; the launch traced here: 1280 us
  waiting for transfers between devices  800 us (62%)
  blocking collectives  143 us (11%)
  starting transfers between devices  101 us (8%)
  local copies, waits for them, and re-layouts  100 us (8%)
  matrix products  89 us (7%)
  other arithmetic  33.6 us (3%)
  between operations  16 us (1%)
    reduce_scatter x5, waiting for transfers between devices, on_device(): lax.psum_scatter(partial_out.astype(jnp.bfloat16), 'tp', scatter_dimensio...  356 us
    reduce_scatter x5, waiting for transfers between devices, on_device(): lax.psum_scatter(partial_in.astype(jnp.bfloat16), 'tp', scatter_dimension...  278 us
    psum x5, blocking collectives, on_device(): stat = lax.psum(jnp.sum(dnorm_local * normed_local, axis=1), 'tp') / D  125 us
    ppermute x1, waiting for transfers between devices, from_behind(): lax.ppermute(array, axis, [(i, (i + by) % peers) for i in range(peers)])  87.7 us
    dot_general x30, matrix products, contract(): lax.dot_general(left, right, (((left_dim,), (right_dim,)), ((), ())), pre...  68.3 us
    all_to_all x9, starting transfers between devices, wrap_the_joints(): n_now = lax.all_to_all(mid_arr, row_axis, 0, 0)  66.3 us
    all_to_all x9, waiting for transfers between devices, wrap_the_joints(): n_now = lax.all_to_all(mid_arr, row_axis, 0, 0)  63.2 us
    slice x1, local copies, waits for them, and re-layouts, on_device(): new_down = averaged[2].reshape(wd.shape)[None, None]  32.7 us
  transfers between devices with their start and end apart: 28, of which 24 were waited for; matrix products, arithmetic and copies ran while one was open for 13% of the time, Pallas kernels for 0%

profile of v1, /device:TPU:66, one launch (start us, length us, event | category | flops | bytes accessed | tf_op | source)
XLA Modules:
  0.0 1283.6 jit_solution(10124385350771374576)
XLA Ops:
  9.8 9.8 all-to-all-start
  19.6 11.5 all-to-all-done
  35.2 72.2 %reduce-scatter.11.cloned.1.call-done = bf16[128,112]{0,1:T(8,128)(2,1)} async-done(((bf16[128,896]{0,1:T(8,128)(2,1)}), bf16[128,112]{0,1:T(8,128)(2,1)}) %reduce-scatter.11.cloned.1.call-update) | async-done | bytes 28688 | tf_op jit(solution)/shard_map/reduce_scatter | solution.py:113
  110.8 3.1 collective-permute-done.3
  114.6 5.9 all-to-all-start.1
  120.5 9.9 all-to-all-done.1
  134.6 72.4 %reduce-scatter.13.cloned.1.call-done = bf16[128,112]{0,1:T(8,128)(2,1)} async-done(((bf16[128,896]{0,1:T(8,128)(2,1)}), bf16[128,112]{0,1:T(8,128)(2,1)}) %reduce-scatter.13.cloned.1.call-update) | async-done | bytes 28688 | tf_op jit(solution)/shard_map/reduce_scatter | solution.py:113
  210.3 3.1 collective-permute-done.4
  214.2 5.9 all-to-all-start.2
  220.1 9.9 all-to-all-done.2
  234.2 72.4 %reduce-scatter.15.cloned.1.call-done = bf16[128,112]{0,1:T(8,128)(2,1)} async-done(((bf16[128,896]{0,1:T(8,128)(2,1)}), bf16[128,112]{0,1:T(8,128)(2,1)}) %reduce-scatter.15.cloned.1.call-update) | async-done | bytes 28688 | tf_op jit(solution)/shard_map/reduce_scatter | solution.py:113
  310.0 3.1 collective-permute-done.5
  314.6 5.9 all-to-all-start.3
  322.4 8.1 all-to-all-done.3
  336.1 70.8 %reduce-scatter.17.cloned.1.call-done = bf16[128,112]{0,1:T(8,128)(2,1)} async-done(((bf16[128,896]{0,1:T(8,128)(2,1)}), bf16[128,112]{0,1:T(8,128)(2,1)}) %reduce-scatter.17.cloned.1.call-update) | async-done | bytes 28688 | tf_op jit(solution)/shard_map/reduce_scatter | solution.py:113
  410.5 3.0 collective-permute-done.6
  415.1 5.9 all-to-all-start.4
  423.1 7.8 all-to-all-done.4
  432.4 5.7 all-to-all-start.5
  442.6 4.9 all-to-all-done.5
  453.5 70.8 %reduce-scatter.21.cloned.1.call-done = bf16[128,112]{0,1:T(8,128)(2,1)} async-done(((bf16[128,896]{0,1:T(8,128)(2,1)}), bf16[128,112]{0,1:T(8,128)(2,1)}) %reduce-scatter.21.cloned.1.call-update) | async-done | bytes 28688 | tf_op jit(solution)/shard_map/reduce_scatter | solution.py:159
  525.2 24.6 %psum.35 = f32[128]{0:T(128)S(1)} all-reduce(f32[128]{0:T(128)S(1)} %fusion.176), channel_id=1, replica_groups=mesh['section'=4,'rep'=8,'tp'=8] {'tp'}, use_global_device_ids=true, to_apply=%region_13.14 | all-reduce | flops 128 | bytes 1024 | tf_op jit(solution)/shard_map/psum | solution.py:163
  550.6 3.3 collective-permute-start.7
  557.1 18.1 %all_to_all.50 = bf16[8,128,112]{1,2,0:T(8,128)(2,1)S(1)} all-to-all(bf16[8,128,112]{1,2,0:T(8,128)(2,1)S(1)} %stack.34), channel_id=1, replica_groups=mesh['section'=4,'rep'=8,'tp'=8] {'tp'}, dimensions={0} | all-to-all | bytes 458752 | tf_op jit(solution)/shard_map/all_to_all | solution.py:39
  580.2 2.7 fusion.172
  583.0 69.0 %reduce-scatter.23.cloned.1.call-done = bf16[128,112]{0,1:T(8,128)(2,1)} async-done(((bf16[128,896]{0,1:T(8,128)(2,1)}), bf16[128,112]{0,1:T(8,128)(2,1)}) %reduce-scatter.23.cloned.1.call-update) | async-done | bytes 28688 | tf_op jit(solution)/shard_map/reduce_scatter | solution.py:159
  653.3 25.2 %psum.36 = f32[128]{0:T(128)} all-reduce(f32[128]{0:T(128)} %fusion.180), channel_id=1, replica_groups=mesh['section'=4,'rep'=8,'tp'=8] {'tp'}, use_global_device_ids=true, to_apply=%region_17.18 | all-reduce | flops 128 | bytes 1024 | tf_op jit(solution)/shard_map/psum | solution.py:163
  680.1 3.3 collective-permute-start.8
  683.4 2.8 fusion.174
  687.5 9.1 all-to-all-start.7
  699.3 2.9 fusion.151
  702.2 3.6 all-to-all-done.7
  710.4 68.3 %reduce-scatter.19.cloned.1.call-done = bf16[128,112]{0,1:T(8,128)(2,1)} async-done(((bf16[128,896]{0,1:T(8,128)(2,1)}), bf16[128,112]{0,1:T(8,128)(2,1)}) %reduce-scatter.19.cloned.1.call-update) | async-done | bytes 28688 | tf_op jit(solution)/shard_map/reduce_scatter | solution.py:113
  783.0 2.8 fusion.149
  785.7 70.2 %reduce-scatter.25.cloned.1.call-done = bf16[128,112]{0,1:T(8,128)(2,1)} async-done(((bf16[128,896]{0,1:T(8,128)(2,1)}), bf16[128,112]{0,1:T(8,128)(2,1)}) %reduce-scatter.25.cloned.1.call-update) | async-done | bytes 28688 | tf_op jit(solution)/shard_map/reduce_scatter | solution.py:159
  856.9 24.6 %psum.37 = f32[128]{0:T(128)S(1)} all-reduce(f32[128]{0:T(128)S(1)} %fusion.184), channel_id=1, replica_groups=mesh['section'=4,'rep'=8,'tp'=8] {'tp'}, use_global_device_ids=true, to_apply=%region_21.22 | all-reduce | flops 128 | bytes 1024 | tf_op jit(solution)/shard_map/psum | solution.py:163
  882.3 3.3 collective-permute-start.9
  889.1 9.1 all-to-all-start.8
  898.3 2.8 fusion.170
  903.6 3.8 all-to-all-done.8
  911.7 2.8 fusion.166
  914.5 2.9 fusion.147
  917.4 67.8 %reduce-scatter.27.cloned.1.call-done = bf16[128,112]{0,1:T(8,128)(2,1)} async-done(((bf16[128,896]{0,1:T(8,128)(2,1)}), bf16[128,112]{0,1:T(8,128)(2,1)}) %reduce-scatter.27.cloned.1.call-update) | async-done | bytes 28688 | tf_op jit(solution)/shard_map/reduce_scatter | solution.py:159
  986.1 25.1 %psum.38 = f32[128]{0:T(128)} all-reduce(f32[128]{0:T(128)S(1)} %fusion.188), channel_id=1, replica_groups=mesh['section'=4,'rep'=8,'tp'=8] {'tp'}, use_global_device_ids=true, to_apply=%region_25.26 | all-reduce | flops 128 | bytes 1024 | tf_op jit(solution)/shard_map/psum | solution.py:163
  1012.7 3.3 collective-permute-start.10
  1016.0 2.8 fusion.160
  1020.1 9.1 all-to-all-start.9
  1031.9 2.9 fusion.145
  1034.8 3.8 all-to-all-done.9
  1042.5 7.5 fusion.21
  1050.0 3.1 copy.56
  1053.2 4.1 fusion.19
  1059.7 3.0 reshape.326
  1062.8 13.2 %stack_reshape.10 = bf16[1,544768]{1,0:T(2,128)(2,1)} reshape(bf16[544768]{0:T(1024)(128)(2,1)S(1)} %reshape.326) | data formatting | bytes 2179072 | tf_op jit(solution)/shard_map/stack;reshape | solution.py:176
  1076.0 4.9 fusion.20
  1082.4 4.0 reshape.328
  1086.4 11.3 stack_reshape.9
  1097.7 7.4 pad_maximum_fusion
  1105.2 143.4 %conditional.2 = (bf16[3,544768]{1,0:T(4,128)(2,1)}, bf16[1,544768]{1,0:T(2,128)(2,1)}, bf16[1,544768]{1,0:T(2,128)(2,1)}, bf16[1,544768]{1,0:T(2,128)(2,1)}, bf...) conditional(s32[]{:T(128)} %clamp.3, ...), branch_computations={%region_30.31_spmd, %region_31.32_spmd, %region_32.33_spmd} | conditional | flops 8171520 | bytes 56655996
  1105.4 10.7 collective-permute-start.2
  1116.1 87.7 %collective-permute-done.2 = bf16[3,544768]{1,0:T(4,128)(2,1)S(1)} collective-permute-done((bf16[3,544768]{1,0:T(4,128)(2,1)S(1)}, bf16[3,544768]{1,0:T(4,128)(2,1)S(1)}, u32[]{:S(2)}, u32[]{:S(2)}) %collective-permute-start.2) | collective-permute-done | bytes 3268640 | tf_op jit(solution)/shard_map/cond/branch_2_fun/ppermute | solution.py:25
  1203.8 2.9 add_multiply_fusion.2
  1206.8 32.7 %fusion.231 = (bf16[544768]{0:T(1024)(128)(2,1)S(1)}, bf16[1,544768]{1,0:T(2,128)(2,1)}, bf16[544768]{0:T(1024)(128)(2,1)}, bf16[1,544768]{1,0:T(2,128)(2,1)}, b...) fusion(bf16[3,544768]{1,0:T(4,128)(2,1)S(1)} %add_multiply_fusion.2), kind=kLoop, calls=%fused_computation.391 | loop fusion | bytes 9805824 | tf_op jit(solution)/shard_map/slice | solution.py:189
  1249.6 25.3 %psum.39 = f32[128]{0:T(128)S(1)} all-reduce(f32[128]{0:T(128)S(1)} %fusion.192), channel_id=1, replica_groups=mesh['section'=4,'rep'=8,'tp'=8] {'tp'}, use_global_device_ids=true, to_apply=%region_29.30 | all-reduce | flops 128 | bytes 1024 | tf_op jit(solution)/shard_map/psum | solution.py:163
  (258 shorter events, 117.5 us)
Async XLA Ops:
  7.2 25.0 %copy-start.3 = (bf16[1,1,896,608]{2,3,1,0:T(8,128)(2,1)S(1)}, bf16[1,1,896,608]{2,3,1,0:T(8,128)(2,1)}, u32[]{:S(2)}) copy-start(bf16[1,1,896,608]{2,3,1,0:T(8,128)(2,1)} %param.18) | copy-start | bytes 3268612
  9.8 23.6 %copy-start.4 = (bf16[1,1,896,608]{2,3,1,0:T(8,128)(2,1)S(1)}, bf16[1,1,896,608]{2,3,1,0:T(8,128)(2,1)}, u32[]{:S(2)}) copy-start(bf16[1,1,896,608]{2,3,1,0:T(8,128)(2,1)} %param.17) | copy-start | bytes 3268612
  9.8 21.3 %all-to-all-start = ((bf16[8,128,112]{1,2,0:T(8,128)(2,1)}), bf16[8,128,112]{1,2,0:T(8,128)(2,1)S(1)}, u32[]{:S(2)}, u32[]{:S(2)}) async-start(bf16[8,128,112]{1,2,0:T(8,128)(2,1)} %stack.28), calls=%async_computation | async-start | bytes 458752 | tf_op jit(solution)/shard_map/all_to_all | solution.py:39
  19.6 87.8 %reduce-scatter.11.cloned.1.call-start = ((), (), s32[]{:S(2)}) async-start(), calls=%async_computation.20 | async-start | bytes 258048 | tf_op jit(solution)/shard_map/reduce_scatter | solution.py:113
  108.1 5.8 collective-permute-start.3
  113.9 16.6 %copy-start.35 = (bf16[128,112]{0,1:T(8,128)(2,1)}, bf16[128,112]{0,1:T(8,128)(2,1)S(1)}, u32[]{:S(2)}) copy-start(bf16[128,112]{0,1:T(8,128)(2,1)S(1)} %bitcast_select_fusion.19) | copy-start | bytes 86020
  114.6 15.8 %all-to-all-start.1 = ((bf16[8,128,112]{1,2,0:T(8,128)(2,1)}), bf16[8,128,112]{1,2,0:T(8,128)(2,1)S(1)}, u32[]{:S(2)}, u32[]{:S(2)}) async-start(bf16[8,128,112]{1,2,0:T(8,128)(2,1)} %stack.29), calls=%async_computation.2 | async-start | bytes 458752 | tf_op jit(solution)/shard_map/all_to_all | solution.py:39
  120.5 86.4 %reduce-scatter.13.cloned.1.call-start = ((), (), s32[]{:S(2)}) async-start(), calls=%async_computation.21 | async-start | bytes 258048 | tf_op jit(solution)/shard_map/reduce_scatter | solution.py:113
  133.3 73.7 %copy-start.36 = (bf16[128,112]{0,1:T(8,128)(2,1)S(1)}, bf16[128,112]{0,1:T(8,128)(2,1)}, u32[]{:S(2)}) copy-start(bf16[128,112]{0,1:T(8,128)(2,1)} %copy-done.35) | copy-start | bytes 86020
  133.3 80.2 %copy-start.42 = (bf16[1,128,112]{1,0,2:T(2,128)(2,1)S(1)}, bf16[1,128,112]{1,0,2:T(2,128)(2,1)}, u32[]{:S(2)}) copy-start(bf16[1,128,112]{1,0,2:T(2,128)(2,1)} %get-tuple-element.119) | copy-start | bytes 86020
  207.7 5.8 collective-permute-start.4
  214.2 15.8 %all-to-all-start.2 = ((bf16[8,128,112]{1,2,0:T(8,128)(2,1)}), bf16[8,128,112]{1,2,0:T(8,128)(2,1)S(1)}, u32[]{:S(2)}, u32[]{:S(2)}) async-start(bf16[8,128,112]{1,2,0:T(8,128)(2,1)} %stack.30), calls=%async_computation.4 | async-start | bytes 458752 | tf_op jit(solution)/shard_map/all_to_all | solution.py:39
  220.1 86.4 %reduce-scatter.15.cloned.1.call-start = ((), (), s32[]{:S(2)}) async-start(), calls=%async_computation.22 | async-start | bytes 258048 | tf_op jit(solution)/shard_map/reduce_scatter | solution.py:113
  230.0 2.8 copy-start.7
  230.2 2.6 copy-start.52
  307.3 13.2 %copy-start.15 = (bf16[2,128,112]{1,2,0:T(8,128)(2,1)}, bf16[2,128,112]{1,2,0:T(8,128)(2,1)S(1)}, u32[]{:S(2)}) copy-start(bf16[2,128,112]{1,2,0:T(8,128)(2,1)S(1)} %get-tuple-element.79) | copy-start | bytes 172036
  307.3 5.8 collective-permute-start.5
  314.6 15.8 %all-to-all-start.3 = ((bf16[8,128,112]{1,2,0:T(8,128)(2,1)}), bf16[8,128,112]{1,2,0:T(8,128)(2,1)S(1)}, u32[]{:S(2)}, u32[]{:S(2)}) async-start(bf16[8,128,112]{1,2,0:T(8,128)(2,1)} %stack.31), calls=%async_computation.6 | async-start | bytes 458752 | tf_op jit(solution)/shard_map/all_to_all | solution.py:39
  320.5 86.4 %reduce-scatter.17.cloned.1.call-start = ((), (), s32[]{:S(2)}) async-start(), calls=%async_computation.23 | async-start | bytes 258048 | tf_op jit(solution)/shard_map/reduce_scatter | solution.py:113
  330.4 2.8 copy-start.8
  330.6 2.6 copy-start.53
  333.3 73.7 %copy-start.16 = (bf16[2,128,112]{1,2,0:T(8,128)(2,1)S(1)}, bf16[2,128,112]{1,2,0:T(8,128)(2,1)}, u32[]{:S(2)}) copy-start(bf16[2,128,112]{1,2,0:T(8,128)(2,1)} %copy-done.15) | copy-start | bytes 172036
  407.8 32.2 %copy-start.17 = (bf16[2,128,112]{1,2,0:T(8,128)(2,1)}, bf16[2,128,112]{1,2,0:T(8,128)(2,1)S(1)}, u32[]{:S(2)}) copy-start(bf16[2,128,112]{1,2,0:T(8,128)(2,1)S(1)} %get-tuple-element.77) | copy-start | bytes 172036
  407.8 5.8 collective-permute-start.6
  415.1 15.8 %all-to-all-start.4 = ((bf16[8,128,112]{1,2,0:T(8,128)(2,1)}), bf16[8,128,112]{1,2,0:T(8,128)(2,1)S(1)}, u32[]{:S(2)}, u32[]{:S(2)}) async-start(bf16[8,128,112]{1,2,0:T(8,128)(2,1)} %stack.32), calls=%async_computation.8 | async-start | bytes 458752 | tf_op jit(solution)/shard_map/all_to_all | solution.py:39
  432.4 15.1 %all-to-all-start.5 = ((bf16[8,128,112]{1,2,0:T(8,128)(2,1)}), bf16[8,128,112]{1,2,0:T(8,128)(2,1)}, u32[]{:S(2)}, u32[]{:S(2)}) async-start(bf16[8,128,112]{1,2,0:T(8,128)(2,1)} %stack.33), calls=%async_computation.10 | async-start | bytes 458752 | tf_op jit(solution)/shard_map/all_to_all | solution.py:39
  438.1 86.2 %reduce-scatter.21.cloned.1.call-start = ((), (), s32[]{:S(2)}) async-start(), calls=%async_computation.25 | async-start | bytes 258048 | tf_op jit(solution)/shard_map/reduce_scatter | solution.py:159
  451.9 97.9 %copy-start.27 = (bf16[1,128,112]{1,0,2:T(2,128)(2,1)S(1)}, bf16[1,128,112]{1,0,2:T(2,128)(2,1)}, u32[]{:S(2)}) copy-start(bf16[1,128,112]{1,0,2:T(2,128)(2,1)} %get-tuple-element.116) | copy-start | bytes 86020
  451.9 104.5 %copy-start.41 = (bf16[1,128,112]{1,0,2:T(2,128)(2,1)S(1)}, bf16[1,128,112]{1,0,2:T(2,128)(2,1)}, u32[]{:S(2)}) copy-start(bf16[1,128,112]{1,0,2:T(2,128)(2,1)} %get-tuple-element.115) | copy-start | bytes 86020
  451.9 200.0 %reduce-scatter.23.cloned.1.call-start = ((), (), s32[]{:S(2)}) async-start(), calls=%async_computation.26 | async-start | bytes 258048 | tf_op jit(solution)/shard_map/reduce_scatter | solution.py:159
  452.0 97.8 %copy-start.48 = (f32[128]{0:T(128)}, f32[128]{0:T(128)S(1)}, u32[]{:S(2)}) copy-start(f32[128]{0:T(128)S(1)} %get-tuple-element.142) | copy-start | bytes 1540
  452.0 104.4 %copy-start.45 = (f32[128]{0:T(128)}, f32[128]{0:T(128)S(1)}, u32[]{:S(2)}) copy-start(f32[128]{0:T(128)S(1)} %get-tuple-element.145) | copy-start | bytes 1540
  452.0 97.7 %copy-start.46 = (f32[128]{0:T(128)}, f32[128]{0:T(128)S(1)}, u32[]{:S(2)}) copy-start(f32[128]{0:T(128)S(1)} %add_sqrt_fusion.2) | copy-start | bytes 1540
  550.6 5.8 collective-permute-start.7
  678.5 7.6 copy-start.40
  680.1 6.0 collective-permute-start.8
  687.5 18.4 %all-to-all-start.7 = ((bf16[8,128,112]{1,2,0:T(8,128)(2,1)}), bf16[8,128,112]{1,2,0:T(8,128)(2,1)}, u32[]{:S(2)}, u32[]{:S(2)}) async-start(bf16[8,128,112]{1,2,0:T(8,128)(2,1)} %stack.35), calls=%async_computation.14 | async-start | bytes 458752 | tf_op jit(solution)/shard_map/all_to_all | solution.py:39
  696.5 82.1 %reduce-scatter.19.cloned.1.call-start = ((), (), s32[]{:S(2)}) async-start(), calls=%async_computation.24 | async-start | bytes 258048 | tf_op jit(solution)/shard_map/reduce_scatter | solution.py:113
  699.3 156.7 %reduce-scatter.25.cloned.1.call-start = ((), (), s32[]{:S(2)}) async-start(), calls=%async_computation.27 | async-start | bytes 258048 | tf_op jit(solution)/shard_map/reduce_scatter | solution.py:159
  785.7 102.6 %copy-start.39 = (bf16[1,128,112]{1,0,2:T(2,128)(2,1)S(1)}, bf16[1,128,112]{1,0,2:T(2,128)(2,1)}, u32[]{:S(2)}) copy-start(bf16[1,128,112]{1,0,2:T(2,128)(2,1)} %get-tuple-element.113) | copy-start | bytes 86020
  882.3 6.0 collective-permute-start.9
  889.1 18.3 %all-to-all-start.8 = ((bf16[8,128,112]{1,2,0:T(8,128)(2,1)}), bf16[8,128,112]{1,2,0:T(8,128)(2,1)S(1)}, u32[]{:S(2)}, u32[]{:S(2)}) async-start(bf16[8,128,112]{1,2,0:T(8,128)(2,1)} %stack.36), calls=%async_computation.16 | async-start | bytes 458752 | tf_op jit(solution)/shard_map/all_to_all | solution.py:39
  898.1 87.1 %reduce-scatter.27.cloned.1.call-start = ((), (), s32[]{:S(2)}) async-start(), calls=%async_computation.28 | async-start | bytes 258048 | tf_op jit(solution)/shard_map/reduce_scatter | solution.py:159
  898.3 2.8 copy-start.24
  1011.2 7.6 copy-start.38
  1012.7 6.1 collective-permute-start.10
  1020.1 18.4 %all-to-all-start.9 = ((bf16[8,128,112]{1,2,0:T(8,128)(2,1)}), bf16[8,128,112]{1,2,0:T(8,128)(2,1)}, u32[]{:S(2)}, u32[]{:S(2)}) async-start(bf16[8,128,112]{1,2,0:T(8,128)(2,1)} %stack.37), calls=%async_computation.18 | async-start | bytes 458752 | tf_op jit(solution)/shard_map/all_to_all | solution.py:39
  1029.2 219.4 %reduce-scatter.29.cloned.1.call-start = ((), (), s32[]{:S(2)}) async-start(), calls=%async_computation.29 | async-start | bytes 258048 | tf_op jit(solution)/shard_map/reduce_scatter | solution.py:159
  1042.4 10.7 copy-start.11
  1042.4 10.7 copy-start.12
  1042.5 10.7 copy-start.13
  1042.5 10.7 copy-start.54
  1042.5 10.7 copy-start.55
  1050.0 3.2 copy-start.9
  1050.0 3.2 copy-start.44
  1050.0 3.2 copy-start.49
  1062.7 13.2 %copy-start.10 = (f32[896,608]{0,1:T(8,128)S(1)}, f32[896,608]{0,1:T(8,128)}, u32[]{:S(2)}) copy-start(f32[896,608]{0,1:T(8,128)} %fusion.174) | copy-start | bytes 6537220
  1062.7 13.2 %copy-start.56 = (bf16[1,1,896,608]{2,3,1,0:T(8,128)(2,1)S(1)}, bf16[1,1,896,608]{2,3,1,0:T(8,128)(2,1)}, u32[]{:S(2)}) copy-start(bf16[1,1,896,608]{2,3,1,0:T(8,128)(2,1)} %param.23) | copy-start | bytes 3268612
  1082.4 15.3 %copy-start.6 = (bf16[1,544768]{1,0:T(2,128)(2,1)S(1)}, bf16[1,544768]{1,0:T(2,128)(2,1)}, u32[]{:S(2)}) copy-start(bf16[1,544768]{1,0:T(2,128)(2,1)} %stack_reshape.10) | copy-start | bytes 3268612
  1086.4 11.4 copy-start.5
  1105.1 169.8 %copy-start.33 = (bf16[128,112]{0,1:T(8,128)(2,1)S(1)}, bf16[128,112]{0,1:T(8,128)(2,1)}, u32[]{:S(2)}) copy-start(bf16[128,112]{0,1:T(8,128)(2,1)} %copy-done.32) | copy-start | bytes 86020
  1105.4 98.5 %collective-permute-start.2 = (bf16[3,544768]{1,0:T(4,128)(2,1)S(1)}, bf16[3,544768]{1,0:T(4,128)(2,1)S(1)}, u32[]{:S(2)}, u32[]{:S(2)}) collective-permute-start(bf16[3,544768]{1,0:T(4,128)(2,1)S(1)} %param.2), channel_id=1, source_target_pairs={{0,32},{8,40},{16,48},{24,56},{32,0},{40,8},{48,16},{56,24},{1,33}... | collective-permute-start | bytes 9805832 | tf_op jit(solution)/shard_map/cond/branch_2_fun/ppermute | solution.py:25
  1206.7 32.7 %copy-start.2 = (bf16[3,544768]{1,0:T(4,128)(2,1)}, bf16[3,544768]{1,0:T(4,128)(2,1)S(1)}, u32[]{:S(2)}) copy-start(bf16[3,544768]{1,0:T(4,128)(2,1)S(1)} %add_multiply_fusion.2) | copy-start | bytes 9805828 | tf_op jit(solution)/shard_map/conditional
  1248.6 27.9 %copy-start.14 = (bf16[1,1,896,608]{2,3,1,0:T(8,128)(2,1)}, bf16[1,1,896,608]{2,3,1,0:T(8,128)(2,1)S(1)}, u32[]{:S(2)}) copy-start(bf16[1,1,896,608]{2,3,1,0:T(8,128)(2,1)S(1)} %get-tuple-element.44) | copy-start | bytes 3268612
  (19 other events, 19.9 us)
Sparse Core Ops, SparseCore 0:
  35.3 71.9 reduce-scatter.10
  134.7 72.1 reduce-scatter.12
  234.3 72.1 reduce-scatter.14
  334.7 72.2 reduce-scatter.16
  452.0 72.1 reduce-scatter.20
  579.6 72.2 reduce-scatter.22
  701.6 76.9 reduce-scatter.18
  782.8 73.0 reduce-scatter.24
  911.8 73.3 reduce-scatter.26
  1042.6 73.2 reduce-scatter.28
